TPU v7x, 32 devices: a whole 2x2x4 slice. The times are simulated.
32 devices in a mesh: ctx: 8 (over z, y), head: 4 (over x, core).
Axes of the slice: x: 2, y: 2, z: 4, core: 2. Of those that a mesh axis runs over, the one named last changes fastest.
Arguments:
- queries: bfloat16 [2048, 4096], P(('ctx', 'head')), may hold values from -6.5 to 6.5
- keys: bfloat16 [2048, 2048], P(('ctx', 'head')), may hold values from -6.5 to 6.5
- values: bfloat16 [2048, 2048], P(('ctx', 'head')), may hold values from -6 to 6
- grad_out: bfloat16 [2048, 4096], P(('ctx', 'head')), may hold values from -6 to 6
- segments: int32 [2048], P('ctx'), may hold values from 0 to 3, never falling along the last dimension, each value on 1 to 1024 neighbouring positions
Outputs:
- attended: bfloat16 [2048, 4096], P(('ctx', 'head'))
- grad_queries: bfloat16 [2048, 4096], P(('ctx', 'head'))
- grad_keys: bfloat16 [2048, 2048], P(('ctx', 'head'))
- grad_values: bfloat16 [2048, 2048], P(('ctx', 'head'))
Inputs may be any that keep to these rules, and one draw needn't show every extreme that they name: `segments`: document numbers never fall along the sequence; each document holds 1 to 1024 tokens.
All inputs are finite; a program needn't handle non-finite values.
Results may differ from a plain program's by a relative error of at most 0.019.
Values may be sent and summed in bfloat16 or wider, within the bound.
No kernel may reach another device: no remote copies, remote signals or barrier semaphores. Data moves between devices by JAX's collectives and lax.ppermute only.
A program may use at most 64 MiB of HBM per device.

v0:
```python
import jax
import jax.numpy as jnp
import numpy as np
from jax import lax
from jax.experimental import pallas as pl
from jax.experimental.pallas import tpu as pltpu
from jax.sharding import Mesh, PartitionSpec as P


QHEADS = 32
KVHEADS = 16
HEAD_DIM = 128
WINDOW = 1024
PER_GROUP = QHEADS // KVHEADS

ATTN_SCALE = 168.0 ** (-0.5)
EXP_SCALE = ATTN_SCALE * 1.4426950408889634
HIDDEN = -1e30
TOGETHER = 0
TILE = 256
F32 = jnp.float32
BF16 = jnp.bfloat16
WHOLE = pl.BlockSpec(memory_space=pltpu.VMEM)
ANYWHERE = pl.BlockSpec(memory_space=pl.ANY)
SCALARS = pl.BlockSpec(memory_space=pltpu.SMEM)


def dot(a, b, contract):
    return lax.dot_general(a, b, ((contract[0], contract[1]), ((), ())), preferred_element_type=F32)


def pack_kernel(groups, q_ref, g_ref, k_ref, v_ref, out_ref, q_sc, g_sc, k_sc, v_sc, hold, in_sem, out_sem):
    qw = PER_GROUP * HEAD_DIM
    kw = HEAD_DIM
    half = groups // 2
    pairs = ((q_ref, q_sc, qw, 0), (g_ref, g_sc, qw, qw), (k_ref, k_sc, kw, 2 * qw), (v_ref, v_sc, kw, 2 * qw + kw))

    def fetch(part):
        return [
            pltpu.make_async_copy(
                ref.at[:, part * half * w : (part + 1) * half * w],
                sc.at[:, part * half * w : (part + 1) * half * w],
                in_sem.at[part, n],
            )
            for n, (ref, sc, w, at) in enumerate(pairs)
        ]

    def emit(j):
        return pltpu.make_async_copy(hold.at[j], out_ref.at[j], out_sem.at[j])

    for part in range(2):
        for copy in fetch(part):
            copy.start()
    for part in range(2):
        for copy in fetch(part):
            copy.wait()
        for j in range(part * half, (part + 1) * half):
            for ref, sc, w, at in pairs:
                hold[j, :, at : at + w] = sc[:, j * w : (j + 1) * w]
            emit(j).start()
    for j in range(groups):
        emit(j).wait()


def unpack_kernel(groups, count, *refs):
    ins, (o_ref, dq_ref, dk_ref, dv_ref) = refs[:count], refs[count:]
    main, side = ins[0], ins[-1]
    qw = PER_GROUP * HEAD_DIM
    kw = HEAD_DIM
    base = 2 * qw if count == 1 else 0
    for j in range(groups):
        o_ref[:, j * qw : (j + 1) * qw] = main[j, :, 0:qw]
        dq_ref[:, j * qw : (j + 1) * qw] = main[j, :, qw : 2 * qw]
        dk_ref[:, j * kw : (j + 1) * kw] = side[j, :, base : base + kw]
        dv_ref[:, j * kw : (j + 1) * kw] = side[j, :, base + kw : base + 2 * kw]


def attention_kernel(rows, prev, split, *refs):
    if prev:
        bounds_ref, ids_ref, x_ref, before_ref, *rest = refs
    else:
        bounds_ref, ids_ref, x_ref, *rest = refs
        before_ref = None
    if split:
        out_ref, own_ref, back_ref, *scratch = rest
        kp_sc, vp_sc, ktp_sc, vtp_sc, sp_sc, ep_sc, dkp_sc, dvp_sc, accp_sc, dqp_sc = scratch[7:]
    else:
        out_ref, *scratch = rest
        own_ref = back_ref = None
    kt_sc, vt_sc, s_sc, e_sc, ds_sc, qs_sc, gs_sc = scratch[:7]
    d = HEAD_DIM
    qw = PER_GROUP * d
    q_tiles = rows // TILE
    prev_tiles = prev // TILE
    wide = PER_GROUP * TILE
    key_at, value_at = 2 * qw, 2 * qw + d

    low_all = lowest_keys(ids_ref[...], q_tiles, bounds_ref[2 * q_tiles])
    lanes = lax.broadcasted_iota(jnp.int32, (1, wide), 1) % TILE
    key_rows = lax.broadcasted_iota(jnp.int32, (TILE, wide), 0)
    for t in range(prev_tiles):
        span = slice(t * TILE, (t + 1) * TILE)
        k, v = before_ref[span, 0:d], before_ref[span, d : 2 * d]
        kp_sc[t], vp_sc[t], ktp_sc[t], vtp_sc[t] = k, v, k.T, v.T
        dkp_sc[t] = jnp.zeros((TILE, d), F32)
        dvp_sc[t] = jnp.zeros((TILE, d), F32)

    for i in range(q_tiles):
        span = slice(i * TILE, (i + 1) * TILE)
        cols = slice(i * wide, (i + 1) * wide)
        reach = slice(0, (i + 1) * TILE)
        kt_sc[:, span] = x_ref[span, key_at : key_at + d].T
        vt_sc[:, span] = x_ref[span, value_at : value_at + d].T
        q = jnp.concatenate([x_ref[span, n * d : (n + 1) * d] for n in range(PER_GROUP)], 0)
        g = jnp.concatenate([x_ref[span, qw + n * d : qw + (n + 1) * d] for n in range(PER_GROUP)], 0)
        low = jnp.concatenate([low_all[i : i + 1]] * PER_GROUP, 1)
        first = jnp.maximum(bounds_ref[i] + prev_tiles, 0)

        top = jnp.full((1, wide), HIDDEN, F32)
        for t in range(i + 1):
            at = slice(t * TILE, (t + 1) * TILE)
            s = dot(x_ref[at, key_at : key_at + d], q, ((1,), (1,)))
            s = jnp.where(key_rows >= low - t * TILE, s, HIDDEN)
            if t == i:
                s = jnp.where(key_rows <= lanes, s, HIDDEN)
            s_sc[at, :] = s
            top = jnp.maximum(top, jnp.max(s, axis=0, keepdims=True))

        def scores(t, top):
            s = dot(kp_sc[t], q, ((1,), (1,)))
            s = jnp.where(key_rows >= low - (t - prev_tiles) * TILE, s, HIDDEN)
            sp_sc[t] = s
            return jnp.maximum(top, jnp.max(s, axis=0, keepdims=True))

        if prev:
            top = lax.fori_loop(first, prev_tiles, scores, top)
        shift = top * EXP_SCALE

        total = jnp.zeros((1, wide), F32)
        for t in range(i + 1):
            at = slice(t * TILE, (t + 1) * TILE)
            e = jnp.exp2(s_sc[at, :] * EXP_SCALE - shift)
            e_sc[at, cols] = e.astype(BF16)
            total = total + jnp.sum(e, axis=0, keepdims=True)
        acc = dot(vt_sc[:, reach], e_sc[reach, cols], ((1,), (0,)))

        def forward(t, total):
            e = jnp.exp2(sp_sc[t] * EXP_SCALE - shift)
            small = e.astype(BF16)
            ep_sc[t] = small
            accp_sc[...] += dot(vtp_sc[t], small, ((1,), (0,)))
            return total + jnp.sum(e, axis=0, keepdims=True)

        if prev:
            accp_sc[...] = acc
            total = lax.fori_loop(first, prev_tiles, forward, total)
            acc = accp_sc[...]
        inverse = 1.0 / total
        attended = (acc * inverse).astype(BF16)
        delta = jnp.sum(attended.astype(F32) * g.T.astype(F32), axis=0, keepdims=True)
        down = jnp.broadcast_to(inverse, (d, wide)).T
        gs_sc[cols, :] = (g.astype(F32) * down).astype(BF16)
        qs_sc[cols, :] = (q.astype(F32) * (down * ATTN_SCALE)).astype(BF16)

        for t in range(i + 1):
            at = slice(t * TILE, (t + 1) * TILE)
            dp = dot(x_ref[at, value_at : value_at + d], g, ((1,), (1,)))
            ds_sc[at, cols] = (e_sc[at, cols].astype(F32) * (dp - delta)).astype(BF16)
        dq = dot(kt_sc[:, reach], ds_sc[reach, cols], ((1,), (0,)))

        def backward(t, carry):
            e = ep_sc[t]
            dp = dot(vp_sc[t], g, ((1,), (1,)))
            ds = (e.astype(F32) * (dp - delta)).astype(BF16)
            dkp_sc[t] += dot(ds, qs_sc[cols, :], ((1,), (0,)))
            dvp_sc[t] += dot(e, gs_sc[cols, :], ((1,), (0,)))
            dqp_sc[...] += dot(ktp_sc[t], ds, ((1,), (0,)))
            return carry

        if prev:
            dqp_sc[...] = dq
            lax.fori_loop(first, prev_tiles, backward, 0)
            dq = dqp_sc[...]
        attended = attended.T
        dq = (dq * (inverse * ATTN_SCALE)).astype(BF16).T
        for n in range(PER_GROUP):
            out_ref[span, n * d : (n + 1) * d] = attended[n * TILE : (n + 1) * TILE]
            out_ref[span, qw + n * d : qw + (n + 1) * d] = dq[n * TILE : (n + 1) * TILE]

    for t in range(q_tiles):
        at = slice(t * TILE, (t + 1) * TILE)
        dk = dot(ds_sc[at, t * wide :], qs_sc[t * wide :, :], ((1,), (0,)))
        dv = dot(e_sc[at, t * wide :], gs_sc[t * wide :, :], ((1,), (0,)))
        if split:
            own_ref[at, 0:d] = dk
            own_ref[at, d : 2 * d] = dv
        else:
            out_ref[at, key_at : key_at + d] = dk.astype(BF16)
            out_ref[at, value_at : value_at + d] = dv.astype(BF16)
    for t in range(prev_tiles):
        back_ref[t * TILE : (t + 1) * TILE, 0:d] = dkp_sc[t].astype(BF16)
        back_ref[t * TILE : (t + 1) * TILE, d : 2 * d] = dvp_sc[t].astype(BF16)


def assemble(parts, subs, sub):
    rows = [None] * len(parts)
    for n, part in enumerate(parts):
        turn, base = n % subs, len(parts) - subs if n < subs else 0
        for p in range(subs):
            seen = rows[base + p]
            rows[base + p] = part if seen is None else jnp.where((sub ^ turn) == p, part, seen)
    return jnp.concatenate(rows, 0)


def decide_kernel(subs, run, blocks, place_ref, *refs):
    count = subs * (2 if blocks > 1 else 1)
    ids_ref, bounds_ref, needed_ref = refs[count:]
    block, sub = place_ref[0], place_ref[1]
    ahead = count - subs
    ids = assemble([ref[...] for ref in refs[:count]], subs, sub).astype(F32)
    ids_ref[...] = ids
    heads = jnp.min(ids, axis=1, keepdims=True)
    tails = jnp.max(ids, axis=1, keepdims=True)
    row = lax.broadcasted_iota(jnp.int32, (count, 1), 0)
    if ahead:
        after = jnp.sum((tails[ahead:] == heads[0:1]).astype(F32))
        needed = jnp.sum((tails[:ahead] == heads[ahead : ahead + 1]).astype(F32))
        if blocks > 2:
            after = 0.0
        needed_ref[0] = jnp.where(block == 0, after, needed).astype(jnp.int32)
        absent = (row < ahead) & (block == 0)
        heads = jnp.where(absent, -1.0, heads)
        tails = jnp.where(absent, -1.0, tails)
    else:
        needed_ref[0] = 0
    reach = WINDOW // run
    for i in range(subs):
        first = jnp.sum((tails < heads[ahead + i : ahead + i + 1]).astype(F32)).astype(jnp.int32)
        middle = jnp.sum((heads < tails[ahead + i : ahead + i + 1]).astype(F32)).astype(jnp.int32)
        bounds_ref[i] = jnp.maximum(first - ahead, i - reach)
        bounds_ref[subs + i] = jnp.maximum(middle - ahead, i + 1 - reach)
    bounds_ref[2 * subs] = block


def lowest_keys(ids, subs, block):
    count, run = ids.shape
    ahead = count - subs
    lane = lax.broadcasted_iota(jnp.int32, (count, run), 1)
    row = lax.broadcasted_iota(jnp.int32, (count, run), 0)
    spot = ((row - ahead) * run + lane).astype(F32)
    turned = pltpu.roll(ids, 1, 1)
    lagged = jnp.concatenate([turned[:1], turned[: count - 1]], 0)
    before = jnp.where(lane == 0, lagged, turned)
    opens = (ids != before) | ((lane == 0) & ((row == 0) | ((row == ahead) & (block == 0))))
    far = -4.0 * run * count
    start = jnp.where(opens, spot, far)
    step = 1
    while step < run:
        start = jnp.maximum(start, jnp.where(lane >= step, pltpu.roll(start, step, 1), far))
        step *= 2
    ends = jnp.max(start, axis=1, keepdims=True)
    best = [jnp.full((1, 1), far, F32)]
    for p in range(count - 1):
        best.append(jnp.maximum(best[-1], ends[p : p + 1]))
    start = jnp.maximum(start, jnp.concatenate(best, 0))
    return jnp.maximum(start, spot - (WINDOW - 1))[ahead:].astype(jnp.int32)


def attend(bounds, ids, x, before):
    rows = x.shape[0]
    prev = 0 if before is None else before.shape[0]
    split = prev > 0
    d = HEAD_DIM
    qw = PER_GROUP * d
    wide = PER_GROUP * TILE
    span = PER_GROUP * rows
    tiles = prev // TILE
    own_scratch = [
        pltpu.VMEM((d, rows), BF16),
        pltpu.VMEM((d, rows), BF16),
        pltpu.VMEM((rows, wide), F32),
        pltpu.VMEM((rows, span), BF16),
        pltpu.VMEM((rows, span), BF16),
        pltpu.VMEM((span, d), BF16),
        pltpu.VMEM((span, d), BF16),
    ]
    prev_scratch = [
        pltpu.VMEM((tiles, TILE, d), BF16),
        pltpu.VMEM((tiles, TILE, d), BF16),
        pltpu.VMEM((tiles, d, TILE), BF16),
        pltpu.VMEM((tiles, d, TILE), BF16),
        pltpu.VMEM((tiles, TILE, wide), F32),
        pltpu.VMEM((tiles, TILE, wide), BF16),
        pltpu.VMEM((tiles, TILE, d), F32),
        pltpu.VMEM((tiles, TILE, d), F32),
        pltpu.VMEM((d, wide), F32),
        pltpu.VMEM((d, wide), F32),
    ]
    if split:
        out_shape = (
            jax.ShapeDtypeStruct((rows, 2 * qw), BF16),
            jax.ShapeDtypeStruct((rows, 2 * d), F32),
            jax.ShapeDtypeStruct((prev, 2 * d), BF16),
        )
        operands = (bounds, ids, x, before)
    else:
        out_shape = (jax.ShapeDtypeStruct((rows, 2 * qw + 2 * d), BF16),)
        operands = (bounds, ids, x)

    def kernel(*refs):
        attention_kernel(rows, prev, split, *refs)

    return pl.pallas_call(
        kernel,
        out_shape=out_shape,
        in_specs=[SCALARS] + [WHOLE] * (len(operands) - 1),
        out_specs=[WHOLE] * len(out_shape),
        scratch_shapes=own_scratch + (prev_scratch if split else []),
        compiler_params=pltpu.CompilerParams(vmem_limit_bytes=40 << 20),
    )(*operands)


def body(queries, keys, values, grad_out, segments):
    d = HEAD_DIM
    qw = PER_GROUP * d
    blocks, subs, heads = (lax.axis_size(a) for a in ("block", "sub", "head"))
    groups = subs * heads
    local = queries.shape[0]
    run = segments.shape[0]
    rows = run * subs
    assert groups == KVHEADS and rows == WINDOW and run == TILE

    packed = pl.pallas_call(
        lambda *refs: pack_kernel(groups, *refs),
        name="pack",
        out_shape=jax.ShapeDtypeStruct((groups, local, 2 * qw + 2 * d), BF16),
        in_specs=[ANYWHERE] * 4,
        out_specs=ANYWHERE,
        scratch_shapes=[
            pltpu.VMEM(queries.shape, BF16),
            pltpu.VMEM(queries.shape, BF16),
            pltpu.VMEM(keys.shape, BF16),
            pltpu.VMEM(keys.shape, BF16),
            pltpu.VMEM((groups, local, 2 * qw + 2 * d), BF16),
            pltpu.SemaphoreType.DMA((2, 4)),
            pltpu.SemaphoreType.DMA((groups,)),
        ],
    )(queries, grad_out, keys, values)
    x = lax.all_to_all(packed, ("sub", "head"), 0, 0, tiled=True).reshape(rows, 2 * qw + 2 * d)

    block = lax.axis_index("block")
    sub = lax.axis_index("sub")
    both = ("block", "sub")
    line = segments.reshape(1, run)

    def turned_ids(back):
        parts = []
        for turn in range(subs):
            route = [
                (((b - back) % blocks) * subs + (s ^ turn), b * subs + s)
                for b in range(blocks)
                for s in range(subs)
            ]
            parts.append(lax.ppermute(line, both, route) if back or turn else line)
        return parts

    parts = turned_ids(0) + (turned_ids(1) if blocks > 1 else [])
    ids, bounds, needed = pl.pallas_call(
        lambda *refs: decide_kernel(subs, run, blocks, *refs),
        name="decide",
        out_shape=(
            jax.ShapeDtypeStruct((len(parts), run), F32),
            jax.ShapeDtypeStruct((2 * subs + 1,), jnp.int32),
            jax.ShapeDtypeStruct((1,), jnp.int32),
        ),
        in_specs=[SCALARS] + [WHOLE] * len(parts),
        out_specs=[WHOLE, SCALARS, SCALARS],
        compiler_params=pltpu.CompilerParams(vmem_limit_bytes=1 << 20),
    )(jnp.stack([block, sub]), *parts)
    needed = needed.reshape(())
    if blocks > 2:
        step = 1
        while step < blocks:
            turned = lax.ppermute(needed, "block", [(i, (i + step) % blocks) for i in range(blocks)])
            needed = jnp.maximum(needed, turned)
            step *= 2

    def swap(value):
        return lax.all_to_all(value, ("sub", "head"), 0, 0, tiled=True)

    def unpack(*parts):
        return pl.pallas_call(
            lambda *refs: unpack_kernel(groups, len(parts), *refs),
            name="unpack",
            out_shape=(
                jax.ShapeDtypeStruct(queries.shape, BF16),
                jax.ShapeDtypeStruct(queries.shape, BF16),
                jax.ShapeDtypeStruct(keys.shape, BF16),
                jax.ShapeDtypeStruct(keys.shape, BF16),
            ),
            in_specs=[WHOLE] * len(parts),
            out_specs=[WHOLE] * 4,
            compiler_params=pltpu.CompilerParams(vmem_limit_bytes=8 << 20),
        )(*parts)

    def alone(x, ids, bounds):
        (out,) = attend(bounds, ids, x, None)
        return unpack(swap(out.reshape(groups, local, 2 * qw + 2 * d)))

    onward = [(i, i + 1) for i in range(blocks - 1)]
    backward = [(i + 1, i) for i in range(blocks - 1)]

    def fetch(count):
        def branch(x):
            tail = x[rows - count * run :, 2 * qw :]
            return jnp.pad(lax.ppermute(tail, "block", onward), ((rows - count * run, 0), (0, 0)))

        return branch

    def give(count):
        at = rows - count * run

        def branch(out, kv, back):
            late = lax.ppermute(back[at:], "block", backward)
            kv = (kv + jnp.pad(late.astype(F32), ((at, 0), (0, 0)))).astype(BF16)
            if 2 * count <= TOGETHER:
                both = jnp.concatenate([out, kv], 1)
                return unpack(swap(both.reshape(groups, local, 2 * qw + 2 * d)))
            main = swap(out.reshape(groups, local, 2 * qw))
            side = swap(kv.reshape(groups, local, 2 * d))
            return unpack(main, side)

        return branch

    def reaching(x, ids, bounds):
        case = jnp.clip(needed - 1, 0, subs - 1)
        before = lax.switch(case, [fetch(c + 1) for c in range(subs)], x)
        out, kv, back = attend(bounds, ids, x, before)
        return lax.switch(case, [give(c + 1) for c in range(subs)], out, kv, back)

    if blocks == 1:
        return alone(x, ids, bounds)
    return lax.cond(needed == 0, alone, reaching, x, ids, bounds)


def solution(mesh):
    shape = dict(mesh.shape)
    devices = np.asarray(mesh.devices)

    def program(queries, keys, values, grad_out, segments):
        run = segments.shape[0] // shape["ctx"]
        subs = WINDOW // run
        fine = Mesh(
            devices.reshape(shape["ctx"] // subs, subs, shape["head"]), ("block", "sub", "head")
        )
        spread = P(("block", "sub", "head"), None)
        return jax.shard_map(
            body,
            mesh=fine,
            in_specs=(spread, spread, spread, spread, P(("block", "sub"))),
            out_specs=(spread, spread, spread, spread),
            check_vma=False,
        )(queries, keys, values, grad_out, segments)

    return program
```

profile of v0, /device:TPU:0, one launch (start us, length us, event | category | flops | bytes accessed | tf_op | source)
XLA Modules:
  0.0 73.7 jit_solution(6546472487524908445)
XLA Ops:
  0.6 2.5 %pack.1 = bf16[16,64,768]{2,1,0:T(8,128)(2,1)} custom-call(bf16[64,4096]{1,0:T(8,128)(2,1)} %refs_0_.1, bf16[64,4096]{1,0:T(8,128)(2,1)} %refs_1_.1, bf16[64,2048]{1,0:T(8,128)(2,1)} %refs_2_.1, bf16[64,2048]{1,0:T(8,128)(2,1)} %refs_3_.1), custom_call_target="tpu_custom_call" | custom-call | tf_op jit(solution)/shard_map/pack/pallas_call | solution.py:333
  3.1 0.0 copy-start
  3.1 6.3 %all-to-all-start.9 = ((bf16[16,64,768]{2,1,0:T(8,128)(2,1)}), bf16[16,64,768]{2,1,0:T(8,128)(2,1)S(1)}, u32[]{:S(2)}, u32[]{:S(2)}) async-start(bf16[16,64,768]{2,1,0:T(8,128)(2,1)} %pack.1), calls=%async_computation.9 | async-start | bytes 3145728 | tf_op jit(solution)/shard_map/all_to_all | solution.py:349
  9.5 0.0 copy-done
  9.5 4.9 %collective-permute-start.14 = (s32[1,256]{1,0:T(1,128)S(1)}, s32[1,256]{1,0:T(1,128)S(1)}, u32[]{:S(2)}, u32[]{:S(2)}) collective-permute-start(s32[1,256]{1,0:T(1,128)S(1)} %bitcast.15), channel_id=1, source_target_pairs={{28,0},{24,4},{20,8},{16,12},{12,16},{8,20},{4,24},{0,28},{29,1},{... | collective-permute-start | bytes 3080 | tf_op jit(solution)/shard_map/ppermute | solution.py:364
  14.4 0.3 collective-permute-start.13
  14.7 0.3 collective-permute-start.12
  15.1 2.3 %collective-permute-start.11 = (s32[1,256]{1,0:T(1,128)S(1)}, s32[1,256]{1,0:T(1,128)S(1)}, u32[]{:S(2)}, u32[]{:S(2)}) collective-permute-start(s32[1,256]{1,0:T(1,128)S(1)} %bitcast.18), channel_id=1, source_target_pairs={{16,0},{20,4},{24,8},{28,12},{0,16},{4,20},{8,24},{12,28},{17,1},{... | collective-permute-start | bytes 3080 | tf_op jit(solution)/shard_map/ppermute | solution.py:364
  17.4 2.3 %collective-permute-start.10 = (s32[1,256]{1,0:T(1,128)S(1)}, s32[1,256]{1,0:T(1,128)S(1)}, u32[]{:S(2)}, u32[]{:S(2)}) collective-permute-start(s32[1,256]{1,0:T(1,128)S(1)} %bitcast.19), channel_id=1, source_target_pairs={{12,0},{8,4},{4,8},{0,12},{28,16},{24,20},{20,24},{16,28},{13,1},{... | collective-permute-start | bytes 3080 | tf_op jit(solution)/shard_map/ppermute | solution.py:364
  19.7 14.0 %collective-permute-done.14.refs_8_ = s32[1,256]{1,0:T(1,128)S(1)} collective-permute-done((s32[1,256]{1,0:T(1,128)S(1)}, s32[1,256]{1,0:T(1,128)S(1)}, u32[]{:S(2)}, u32[]{:S(2)}) %collective-permute-start.14) | collective-permute-done | bytes 1056 | tf_op jit(solution)/shard_map/ppermute | solution.py:364
  33.7 0.0 collective-permute-start.9
  33.7 0.0 collective-permute-done.13.refs_7_
  33.7 0.6 collective-permute-start.8
  34.2 0.1 pad_add_fusion.refs_0_
  34.3 0.0 collective-permute-done.12.refs_6_
  34.3 0.0 collective-permute-done.11.refs_5_
  34.3 0.0 collective-permute-done.10.refs_4_
  34.3 2.9 %collective-permute-done.9.refs_3_ = s32[1,256]{1,0:T(1,128)S(1)} collective-permute-done((s32[1,256]{1,0:T(1,128)S(1)}, s32[1,256]{1,0:T(1,128)S(1)}, u32[]{:S(2)}, u32[]{:S(2)}) %collective-permute-start.9) | collective-permute-done | bytes 1056 | tf_op jit(solution)/shard_map/ppermute | solution.py:364
  37.2 0.0 collective-permute-done.8.refs_2_
  37.3 1.4 %decide.1 = (f32[8,256]{1,0:T(8,128)S(1)}, s32[9]{0:T(128)S(1)}, s32[1]{0:T(128)}) custom-call(s32[2]{0:T(128)S(1)} %pad_add_fusion.refs_0_, s32[1,256]{1,0:T(1,128)S(1)} %bitcast.22, s32[1,256]{1,0:T(1,128)S(1)} %collective-permute-done.8.refs_2_, s32[1,256]{1,0:T(1,128)S(1)} %collective-permute-done.9.refs_3_, ...), custom_call_target="tpu_custom_call" | custom-call | tf_op jit(solution)/shard_map/decide/pallas_call | solution.py:368
  39.3 0.0 all-to-all-done.9
  39.3 34.4 %conditional.3 = ((bf16[64,4096]{1,0:T(8,128)(2,1)}, bf16[64,4096]{1,0:T(8,128)(2,1)}, bf16[64,2048]{1,0:T(8,128)(2,1)}, bf16[64,2048]{1,0:T(8,128)(2,1)})) conditional(s32[]{:T(128)} %convert_element_type.33, (s32[]{:T(128)}, bf16[1024,768]{1,0:T(8,128)(2,1)S(1)}, s32[9]{0:T(128)S(1)}, f32[8,256]{1,0:T(8,128)S(1)}) %tuple.63, (s32[9]{0:T(128)S(1)}, ...), branch_computations={%region_0.9_spmd, %region_9.10_spmd} | conditional | flops 786436 | bytes 10748078 | solution.py:443
  39.5 6.8 %branch_1_fun.1 = bf16[1024,768]{1,0:T(8,128)(2,1)S(1)} custom-call(s32[9]{0:T(128)S(1)} %get-tuple-element.66.refs_0_, f32[8,256]{1,0:T(8,128)S(1)} %get-tuple-element.67.refs_1_, bf16[1024,768]{1,0:T(8,128)(2,1)S(1)} %get-tuple-element.68.refs_2_), custom_call_target="tpu_custom_call" | custom-call | tf_op jit(solution)/shard_map/cond/branch_1_fun/pallas_call | solution.py:313
  46.3 26.1 %all_to_all.49.refs_0_ = bf16[16,64,768]{2,1,0:T(8,128)(2,1)S(1)} all-to-all(bf16[16,64,768]{2,1,0:T(8,128)(2,1)S(1)} %bitcast.14), channel_id=1, replica_groups=mesh['block'=2,'sub'=4,'head'=4] {'sub','head'}, dimensions={0} | all-to-all | bytes 3145728 | tf_op jit(solution)/shard_map/cond/branch_1_fun/all_to_all | solution.py:389
  72.3 1.4 %unpack.9 = (bf16[64,4096]{1,0:T(8,128)(2,1)}, bf16[64,4096]{1,0:T(8,128)(2,1)}, bf16[64,2048]{1,0:T(8,128)(2,1)}, bf16[64,2048]{1,0:T(8,128)(2,1)}) custom-call(bf16[16,64,768]{2,1,0:T(8,128)(2,1)S(1)} %all_to_all.49.refs_0_), custom_call_target="tpu_custom_call" | custom-call | tf_op jit(solution)/shard_map/cond/branch_1_fun/unpack/pallas_call | solution.py:392
Async XLA Ops:
  3.1 6.3 %copy-start = (s32[256]{0:T(256)S(1)}, s32[256]{0:T(256)}, u32[]{:S(2)}) copy-start(s32[256]{0:T(256)} %param.19) | copy-start | bytes 3076
  3.1 36.1 %all-to-all-start.9 = ((bf16[16,64,768]{2,1,0:T(8,128)(2,1)}), bf16[16,64,768]{2,1,0:T(8,128)(2,1)S(1)}, u32[]{:S(2)}, u32[]{:S(2)}) async-start(bf16[16,64,768]{2,1,0:T(8,128)(2,1)} %pack.1), calls=%async_computation.9 | async-start | bytes 3145728 | tf_op jit(solution)/shard_map/all_to_all | solution.py:349
  9.5 24.2 %collective-permute-start.14 = (s32[1,256]{1,0:T(1,128)S(1)}, s32[1,256]{1,0:T(1,128)S(1)}, u32[]{:S(2)}, u32[]{:S(2)}) collective-permute-start(s32[1,256]{1,0:T(1,128)S(1)} %bitcast.15), channel_id=1, source_target_pairs={{28,0},{24,4},{20,8},{16,12},{12,16},{8,20},{4,24},{0,28},{29,1},{... | collective-permute-start | bytes 3080 | tf_op jit(solution)/shard_map/ppermute | solution.py:364
  14.4 19.3 %collective-permute-start.13 = (s32[1,256]{1,0:T(1,128)S(1)}, s32[1,256]{1,0:T(1,128)S(1)}, u32[]{:S(2)}, u32[]{:S(2)}) collective-permute-start(s32[1,256]{1,0:T(1,128)S(1)} %bitcast.16), channel_id=1, source_target_pairs={{24,0},{28,4},{16,8},{20,12},{8,16},{12,20},{0,24},{4,28},{25,1},{... | collective-permute-start | bytes 3080 | tf_op jit(solution)/shard_map/ppermute | solution.py:364
  14.7 19.6 %collective-permute-start.12 = (s32[1,256]{1,0:T(1,128)S(1)}, s32[1,256]{1,0:T(1,128)S(1)}, u32[]{:S(2)}, u32[]{:S(2)}) collective-permute-start(s32[1,256]{1,0:T(1,128)S(1)} %bitcast.17), channel_id=1, source_target_pairs={{20,0},{16,4},{28,8},{24,12},{4,16},{0,20},{12,24},{8,28},{21,1},{... | collective-permute-start | bytes 3080 | tf_op jit(solution)/shard_map/ppermute | solution.py:364
  15.1 19.3 %collective-permute-start.11 = (s32[1,256]{1,0:T(1,128)S(1)}, s32[1,256]{1,0:T(1,128)S(1)}, u32[]{:S(2)}, u32[]{:S(2)}) collective-permute-start(s32[1,256]{1,0:T(1,128)S(1)} %bitcast.18), channel_id=1, source_target_pairs={{16,0},{20,4},{24,8},{28,12},{0,16},{4,20},{8,24},{12,28},{17,1},{... | collective-permute-start | bytes 3080 | tf_op jit(solution)/shard_map/ppermute | solution.py:364
  17.4 16.9 %collective-permute-start.10 = (s32[1,256]{1,0:T(1,128)S(1)}, s32[1,256]{1,0:T(1,128)S(1)}, u32[]{:S(2)}, u32[]{:S(2)}) collective-permute-start(s32[1,256]{1,0:T(1,128)S(1)} %bitcast.19), channel_id=1, source_target_pairs={{12,0},{8,4},{4,8},{0,12},{28,16},{24,20},{20,24},{16,28},{13,1},{... | collective-permute-start | bytes 3080 | tf_op jit(solution)/shard_map/ppermute | solution.py:364
  33.7 3.6 %collective-permute-start.9 = (s32[1,256]{1,0:T(1,128)S(1)}, s32[1,256]{1,0:T(1,128)S(1)}, u32[]{:S(2)}, u32[]{:S(2)}) collective-permute-start(s32[1,256]{1,0:T(1,128)S(1)} %bitcast.20), channel_id=1, source_target_pairs={{8,0},{12,4},{0,8},{4,12},{24,16},{28,20},{16,24},{20,28},{9,1},{1... | collective-permute-start | bytes 3080 | tf_op jit(solution)/shard_map/ppermute | solution.py:364
  33.7 3.6 %collective-permute-start.8 = (s32[1,256]{1,0:T(1,128)S(1)}, s32[1,256]{1,0:T(1,128)S(1)}, u32[]{:S(2)}, u32[]{:S(2)}) collective-permute-start(s32[1,256]{1,0:T(1,128)S(1)} %bitcast.21), channel_id=1, source_target_pairs={{4,0},{0,4},{12,8},{8,12},{20,16},{16,20},{28,24},{24,28},{5,1},{1... | collective-permute-start | bytes 3080 | tf_op jit(solution)/shard_map/ppermute | solution.py:364
where the time goes:
time: 73.9 us; the launch traced here: 73.7 us
  blocking collectives  26.1 us (35%)
  starting transfers between devices  17.1 us (23%)
  waiting for transfers between devices  16.9 us (23%)
  Pallas kernels  12 us (16%)
  between operations  1.31 us (2%)
    all_to_all x1, blocking collectives, swap(): return lax.all_to_all(value, ('sub', 'head'), 0, 0, tiled=True)  26.1 us
    ppermute x7, waiting for transfers between devices, turned_ids(): parts.append(lax.ppermute(line, both, route) if back or turn else line)  16.9 us
    ppermute x7, starting transfers between devices, turned_ids(): parts.append(lax.ppermute(line, both, route) if back or turn else line)  10.8 us
    pallas_call x1, Pallas kernels, attend(): pl.pallas_call(kernel, out_shape=out_shape, in_specs=[SCALARS] + [WHOLE]...  6.78 us
    all_to_all x1, starting transfers between devices, body(): lax.all_to_all(packed, ('sub', 'head'), 0, 0, tiled=True)  6.33 us
    pallas_call x1, Pallas kernels, body(): pl.pallas_call(lambda *refs: pack_kernel(groups, *refs), name='pack', out...  2.49 us
  transfers between devices with their start and end apart: 8, of which 2 were waited for; matrix products, arithmetic and copies ran while one was open for 0% of the time, Pallas kernels for 2%

commit v1 on v0

--- a/solution.py
+++ b/solution.py
@@ -16,7 +16,7 @@
 ATTN_SCALE = 168.0 ** (-0.5)
 EXP_SCALE = ATTN_SCALE * 1.4426950408889634
 HIDDEN = -1e30
-TOGETHER = 0
+TOGETHER = 2
 TILE = 256
 F32 = jnp.float32
 BF16 = jnp.bfloat16
@@ -83,11 +83,11 @@
         before_ref = None
     if split:
         out_ref, own_ref, back_ref, *scratch = rest
-        kp_sc, vp_sc, ktp_sc, vtp_sc, sp_sc, ep_sc, dkp_sc, dvp_sc, accp_sc, dqp_sc = scratch[7:]
+        kp_sc, vp_sc, ktp_sc, vtp_sc, sp_sc, ep_sc, dkp_sc, dvp_sc, accp_sc, dqp_sc = scratch[9:]
     else:
         out_ref, *scratch = rest
         own_ref = back_ref = None
-    kt_sc, vt_sc, s_sc, e_sc, ds_sc, qs_sc, gs_sc = scratch[:7]
+    kt_sc, vt_sc, s_sc, e_sc, ds_sc, qs_sc, gs_sc, dkt_sc, dvt_sc = scratch[:9]
     d = HEAD_DIM
     qw = PER_GROUP * d
     q_tiles = rows // TILE
@@ -102,15 +102,28 @@
         span = slice(t * TILE, (t + 1) * TILE)
         k, v = before_ref[span, 0:d], before_ref[span, d : 2 * d]
         kp_sc[t], vp_sc[t], ktp_sc[t], vtp_sc[t] = k, v, k.T, v.T
-        dkp_sc[t] = jnp.zeros((TILE, d), F32)
-        dvp_sc[t] = jnp.zeros((TILE, d), F32)
+        dkp_sc[t] = jnp.zeros((d, TILE), F32)
+        dvp_sc[t] = jnp.zeros((d, TILE), F32)
+
+    def collect(i, t):
+        at = slice(t * TILE, (t + 1) * TILE)
+        cols = slice(i * wide, (i + 1) * wide)
+        dk = dot(qs_sc[:, cols], ds_sc[at, cols], ((1,), (1,)))
+        dv = dot(gs_sc[:, cols], e_sc[at, cols], ((1,), (1,)))
+        if t == i:
+            dkt_sc[:, at] = dk
+            dvt_sc[:, at] = dv
+        else:
+            dkt_sc[:, at] += dk
+            dvt_sc[:, at] += dv
 
     for i in range(q_tiles):
         span = slice(i * TILE, (i + 1) * TILE)
         cols = slice(i * wide, (i + 1) * wide)
         reach = slice(0, (i + 1) * TILE)
         kt_sc[:, span] = x_ref[span, key_at : key_at + d].T
-        vt_sc[:, span] = x_ref[span, value_at : value_at + d].T
+        vt_sc[0:d, span] = x_ref[span, value_at : value_at + d].T
+        vt_sc[d:, span] = jnp.ones((16, TILE), BF16)
         q = jnp.concatenate([x_ref[span, n * d : (n + 1) * d] for n in range(PER_GROUP)], 0)
         g = jnp.concatenate([x_ref[span, qw + n * d : qw + (n + 1) * d] for n in range(PER_GROUP)], 0)
         low = jnp.concatenate([low_all[i : i + 1]] * PER_GROUP, 1)
@@ -136,13 +149,15 @@
             top = lax.fori_loop(first, prev_tiles, scores, top)
         shift = top * EXP_SCALE
 
-        total = jnp.zeros((1, wide), F32)
         for t in range(i + 1):
             at = slice(t * TILE, (t + 1) * TILE)
             e = jnp.exp2(s_sc[at, :] * EXP_SCALE - shift)
             e_sc[at, cols] = e.astype(BF16)
-            total = total + jnp.sum(e, axis=0, keepdims=True)
+            if t < i:
+                collect(i - 1, t)
         acc = dot(vt_sc[:, reach], e_sc[reach, cols], ((1,), (0,)))
+        total = acc[d : d + 1]
+        acc = acc[:d]
 
         def forward(t, total):
             e = jnp.exp2(sp_sc[t] * EXP_SCALE - shift)
@@ -157,23 +172,23 @@
             acc = accp_sc[...]
         inverse = 1.0 / total
         attended = (acc * inverse).astype(BF16)
-        delta = jnp.sum(attended.astype(F32) * g.T.astype(F32), axis=0, keepdims=True)
-        down = jnp.broadcast_to(inverse, (d, wide)).T
-        gs_sc[cols, :] = (g.astype(F32) * down).astype(BF16)
-        qs_sc[cols, :] = (q.astype(F32) * (down * ATTN_SCALE)).astype(BF16)
+        gt = g.T.astype(F32)
+        delta = jnp.sum(attended.astype(F32) * gt, axis=0, keepdims=True)
+        gs_sc[:, cols] = (gt * inverse).astype(BF16)
+        qs_sc[:, cols] = (q.T.astype(F32) * (inverse * ATTN_SCALE)).astype(BF16)
 
         for t in range(i + 1):
             at = slice(t * TILE, (t + 1) * TILE)
             dp = dot(x_ref[at, value_at : value_at + d], g, ((1,), (1,)))
-            ds_sc[at, cols] = (e_sc[at, cols].astype(F32) * (dp - delta)).astype(BF16)
+            ds_sc[at, cols] = e_sc[at, cols] * (dp - delta).astype(BF16)
         dq = dot(kt_sc[:, reach], ds_sc[reach, cols], ((1,), (0,)))
 
         def backward(t, carry):
             e = ep_sc[t]
             dp = dot(vp_sc[t], g, ((1,), (1,)))
-            ds = (e.astype(F32) * (dp - delta)).astype(BF16)
-            dkp_sc[t] += dot(ds, qs_sc[cols, :], ((1,), (0,)))
-            dvp_sc[t] += dot(e, gs_sc[cols, :], ((1,), (0,)))
+            ds = e * (dp - delta).astype(BF16)
+            dkp_sc[t] += dot(qs_sc[:, cols], ds, ((1,), (1,)))
+            dvp_sc[t] += dot(gs_sc[:, cols], e, ((1,), (1,)))
             dqp_sc[...] += dot(ktp_sc[t], ds, ((1,), (0,)))
             return carry
 
@@ -189,8 +204,9 @@
 
     for t in range(q_tiles):
         at = slice(t * TILE, (t + 1) * TILE)
-        dk = dot(ds_sc[at, t * wide :], qs_sc[t * wide :, :], ((1,), (0,)))
-        dv = dot(e_sc[at, t * wide :], gs_sc[t * wide :, :], ((1,), (0,)))
+        collect(q_tiles - 1, t)
+        dk = dkt_sc[:, at].T
+        dv = dvt_sc[:, at].T
         if split:
             own_ref[at, 0:d] = dk
             own_ref[at, d : 2 * d] = dv
@@ -198,8 +214,8 @@
             out_ref[at, key_at : key_at + d] = dk.astype(BF16)
             out_ref[at, value_at : value_at + d] = dv.astype(BF16)
     for t in range(prev_tiles):
-        back_ref[t * TILE : (t + 1) * TILE, 0:d] = dkp_sc[t].astype(BF16)
-        back_ref[t * TILE : (t + 1) * TILE, d : 2 * d] = dvp_sc[t].astype(BF16)
+        back_ref[t * TILE : (t + 1) * TILE, 0:d] = dkp_sc[t].T.astype(BF16)
+        back_ref[t * TILE : (t + 1) * TILE, d : 2 * d] = dvp_sc[t].T.astype(BF16)
 
 
 def assemble(parts, subs, sub):
@@ -277,12 +293,14 @@
     tiles = prev // TILE
     own_scratch = [
         pltpu.VMEM((d, rows), BF16),
-        pltpu.VMEM((d, rows), BF16),
+        pltpu.VMEM((d + 16, rows), BF16),
         pltpu.VMEM((rows, wide), F32),
         pltpu.VMEM((rows, span), BF16),
         pltpu.VMEM((rows, span), BF16),
-        pltpu.VMEM((span, d), BF16),
-        pltpu.VMEM((span, d), BF16),
+        pltpu.VMEM((d, span), BF16),
+        pltpu.VMEM((d, span), BF16),
+        pltpu.VMEM((d, rows), F32),
+        pltpu.VMEM((d, rows), F32),
     ]
     prev_scratch = [
         pltpu.VMEM((tiles, TILE, d), BF16),
@@ -291,8 +309,8 @@
         pltpu.VMEM((tiles, d, TILE), BF16),
         pltpu.VMEM((tiles, TILE, wide), F32),
         pltpu.VMEM((tiles, TILE, wide), BF16),
-        pltpu.VMEM((tiles, TILE, d), F32),
-        pltpu.VMEM((tiles, TILE, d), F32),
+        pltpu.VMEM((tiles, d, TILE), F32),
+        pltpu.VMEM((tiles, d, TILE), F32),
         pltpu.VMEM((d, wide), F32),
         pltpu.VMEM((d, wide), F32),
     ]

time: 73.9 us -> 73.4 us (level)
  no operation moved by 1% of the time
where the time goes in v1:
time: 73.4 us; the launch traced here: 73.2 us
  blocking collectives  26 us (35%)
  starting transfers between devices  17.1 us (23%)
  waiting for transfers between devices  16.9 us (23%)
  Pallas kernels  11.5 us (16%)
  between operations  1.3 us (2%)
    all_to_all x1, blocking collectives, swap(): return lax.all_to_all(value, ('sub', 'head'), 0, 0, tiled=True)  26 us
    ppermute x7, waiting for transfers between devices, turned_ids(): parts.append(lax.ppermute(line, both, route) if back or turn else line)  16.9 us
    ppermute x7, starting transfers between devices, turned_ids(): parts.append(lax.ppermute(line, both, route) if back or turn else line)  10.8 us
    all_to_all x1, starting transfers between devices, body(): lax.all_to_all(packed, ('sub', 'head'), 0, 0, tiled=True)  6.33 us
    pallas_call x1, Pallas kernels, attend(): pl.pallas_call(kernel, out_shape=out_shape, in_specs=[SCALARS] + [WHOLE]...  6.3 us
    pallas_call x1, Pallas kernels, body(): pl.pallas_call(lambda *refs: pack_kernel(groups, *refs), name='pack', out...  2.5 us
  transfers between devices with their start and end apart: 8, of which 2 were waited for; matrix products, arithmetic and copies ran while one was open for 0% of the time, Pallas kernels for 2%

profile of v1, /device:TPU:0, one launch (start us, length us, event | category | flops | bytes accessed | tf_op | source)
XLA Modules:
  0.0 73.2 jit_solution(8535650445531184867)
XLA Ops:
  0.6 2.5 %pack.1 = bf16[16,64,768]{2,1,0:T(8,128)(2,1)} custom-call(bf16[64,4096]{1,0:T(8,128)(2,1)} %refs_0_.1, bf16[64,4096]{1,0:T(8,128)(2,1)} %refs_1_.1, bf16[64,2048]{1,0:T(8,128)(2,1)} %refs_2_.1, bf16[64,2048]{1,0:T(8,128)(2,1)} %refs_3_.1), custom_call_target="tpu_custom_call" | custom-call | tf_op jit(solution)/shard_map/pack/pallas_call | solution.py:351
  3.1 0.0 copy-start
  3.2 6.3 %all-to-all-start.8 = ((bf16[16,64,768]{2,1,0:T(8,128)(2,1)}), bf16[16,64,768]{2,1,0:T(8,128)(2,1)S(1)}, u32[]{:S(2)}, u32[]{:S(2)}) async-start(bf16[16,64,768]{2,1,0:T(8,128)(2,1)} %pack.1), calls=%async_computation.8 | async-start | bytes 3145728 | tf_op jit(solution)/shard_map/all_to_all | solution.py:367
  9.5 0.0 copy-done
  9.5 4.9 %collective-permute-start.14 = (s32[1,256]{1,0:T(1,128)S(1)}, s32[1,256]{1,0:T(1,128)S(1)}, u32[]{:S(2)}, u32[]{:S(2)}) collective-permute-start(s32[1,256]{1,0:T(1,128)S(1)} %bitcast.14), channel_id=1, source_target_pairs={{28,0},{24,4},{20,8},{16,12},{12,16},{8,20},{4,24},{0,28},{29,1},{... | collective-permute-start | bytes 3080 | tf_op jit(solution)/shard_map/ppermute | solution.py:382
  14.4 0.3 collective-permute-start.13
  14.7 0.3 collective-permute-start.12
  15.1 2.3 %collective-permute-start.11 = (s32[1,256]{1,0:T(1,128)S(1)}, s32[1,256]{1,0:T(1,128)S(1)}, u32[]{:S(2)}, u32[]{:S(2)}) collective-permute-start(s32[1,256]{1,0:T(1,128)S(1)} %bitcast.17), channel_id=1, source_target_pairs={{16,0},{20,4},{24,8},{28,12},{0,16},{4,20},{8,24},{12,28},{17,1},{... | collective-permute-start | bytes 3080 | tf_op jit(solution)/shard_map/ppermute | solution.py:382
  17.4 2.3 %collective-permute-start.10 = (s32[1,256]{1,0:T(1,128)S(1)}, s32[1,256]{1,0:T(1,128)S(1)}, u32[]{:S(2)}, u32[]{:S(2)}) collective-permute-start(s32[1,256]{1,0:T(1,128)S(1)} %bitcast.18), channel_id=1, source_target_pairs={{12,0},{8,4},{4,8},{0,12},{28,16},{24,20},{20,24},{16,28},{13,1},{... | collective-permute-start | bytes 3080 | tf_op jit(solution)/shard_map/ppermute | solution.py:382
  19.7 14.0 %collective-permute-done.14.refs_8_ = s32[1,256]{1,0:T(1,128)S(1)} collective-permute-done((s32[1,256]{1,0:T(1,128)S(1)}, s32[1,256]{1,0:T(1,128)S(1)}, u32[]{:S(2)}, u32[]{:S(2)}) %collective-permute-start.14) | collective-permute-done | bytes 1056 | tf_op jit(solution)/shard_map/ppermute | solution.py:382
  33.7 0.0 collective-permute-start.9
  33.7 0.0 collective-permute-done.13.refs_7_
  33.7 0.6 collective-permute-start.8
  34.3 0.1 pad_add_fusion.refs_0_
  34.3 0.0 collective-permute-done.12.refs_6_
  34.3 0.0 collective-permute-done.11.refs_5_
  34.3 0.0 collective-permute-done.10.refs_4_
  34.3 2.9 %collective-permute-done.9.refs_3_ = s32[1,256]{1,0:T(1,128)S(1)} collective-permute-done((s32[1,256]{1,0:T(1,128)S(1)}, s32[1,256]{1,0:T(1,128)S(1)}, u32[]{:S(2)}, u32[]{:S(2)}) %collective-permute-start.9) | collective-permute-done | bytes 1056 | tf_op jit(solution)/shard_map/ppermute | solution.py:382
  37.3 0.0 collective-permute-done.8.refs_2_
  37.3 1.4 %decide.1 = (f32[8,256]{1,0:T(8,128)S(1)}, s32[9]{0:T(128)S(1)}, s32[1]{0:T(128)}) custom-call(s32[2]{0:T(128)S(1)} %pad_add_fusion.refs_0_, s32[1,256]{1,0:T(1,128)S(1)} %bitcast.21, s32[1,256]{1,0:T(1,128)S(1)} %collective-permute-done.8.refs_2_, s32[1,256]{1,0:T(1,128)S(1)} %collective-permute-done.9.refs_3_, ...), custom_call_target="tpu_custom_call" | custom-call | tf_op jit(solution)/shard_map/decide/pallas_call | solution.py:386
  39.3 0.0 all-to-all-done.8
  39.3 33.9 %conditional.3 = ((bf16[64,4096]{1,0:T(8,128)(2,1)}, bf16[64,4096]{1,0:T(8,128)(2,1)}, bf16[64,2048]{1,0:T(8,128)(2,1)}, bf16[64,2048]{1,0:T(8,128)(2,1)})) conditional(s32[]{:T(128)} %convert_element_type.33, (s32[]{:T(128)}, bf16[1024,768]{1,0:T(8,128)(2,1)S(1)}, s32[9]{0:T(128)S(1)}, f32[8,256]{1,0:T(8,128)S(1)}) %tuple.63, (s32[9]{0:T(128)S(1)}, ...), branch_computations={%region_0.9_spmd, %region_9.10_spmd} | conditional | flops 3932164 | bytes 12058822 | solution.py:461
  39.5 6.3 %branch_1_fun.1 = bf16[1024,768]{1,0:T(8,128)(2,1)S(1)} custom-call(s32[9]{0:T(128)S(1)} %get-tuple-element.66.refs_0_, f32[8,256]{1,0:T(8,128)S(1)} %get-tuple-element.67.refs_1_, bf16[1024,768]{1,0:T(8,128)(2,1)S(1)} %get-tuple-element.68.refs_2_), custom_call_target="tpu_custom_call" | custom-call | tf_op jit(solution)/shard_map/cond/branch_1_fun/pallas_call | solution.py:331
  45.8 26.0 %all_to_all.44.refs_0_ = bf16[16,64,768]{2,1,0:T(8,128)(2,1)S(1)} all-to-all(bf16[16,64,768]{2,1,0:T(8,128)(2,1)S(1)} %bitcast.13), channel_id=1, replica_groups=mesh['block'=2,'sub'=4,'head'=4] {'sub','head'}, dimensions={0} | all-to-all | bytes 3145728 | tf_op jit(solution)/shard_map/cond/branch_1_fun/all_to_all | solution.py:407
  71.8 1.4 %unpack.9 = (bf16[64,4096]{1,0:T(8,128)(2,1)}, bf16[64,4096]{1,0:T(8,128)(2,1)}, bf16[64,2048]{1,0:T(8,128)(2,1)}, bf16[64,2048]{1,0:T(8,128)(2,1)}) custom-call(bf16[16,64,768]{2,1,0:T(8,128)(2,1)S(1)} %all_to_all.44.refs_0_), custom_call_target="tpu_custom_call" | custom-call | tf_op jit(solution)/shard_map/cond/branch_1_fun/unpack/pallas_call | solution.py:410
Async XLA Ops:
  3.1 6.3 %copy-start = (s32[256]{0:T(256)S(1)}, s32[256]{0:T(256)}, u32[]{:S(2)}) copy-start(s32[256]{0:T(256)} %param.19) | copy-start | bytes 3076
  3.2 36.1 %all-to-all-start.8 = ((bf16[16,64,768]{2,1,0:T(8,128)(2,1)}), bf16[16,64,768]{2,1,0:T(8,128)(2,1)S(1)}, u32[]{:S(2)}, u32[]{:S(2)}) async-start(bf16[16,64,768]{2,1,0:T(8,128)(2,1)} %pack.1), calls=%async_computation.8 | async-start | bytes 3145728 | tf_op jit(solution)/shard_map/all_to_all | solution.py:367
  9.5 24.2 %collective-permute-start.14 = (s32[1,256]{1,0:T(1,128)S(1)}, s32[1,256]{1,0:T(1,128)S(1)}, u32[]{:S(2)}, u32[]{:S(2)}) collective-permute-start(s32[1,256]{1,0:T(1,128)S(1)} %bitcast.14), channel_id=1, source_target_pairs={{28,0},{24,4},{20,8},{16,12},{12,16},{8,20},{4,24},{0,28},{29,1},{... | collective-permute-start | bytes 3080 | tf_op jit(solution)/shard_map/ppermute | solution.py:382
  14.4 19.3 %collective-permute-start.13 = (s32[1,256]{1,0:T(1,128)S(1)}, s32[1,256]{1,0:T(1,128)S(1)}, u32[]{:S(2)}, u32[]{:S(2)}) collective-permute-start(s32[1,256]{1,0:T(1,128)S(1)} %bitcast.15), channel_id=1, source_target_pairs={{24,0},{28,4},{16,8},{20,12},{8,16},{12,20},{0,24},{4,28},{25,1},{... | collective-permute-start | bytes 3080 | tf_op jit(solution)/shard_map/ppermute | solution.py:382
  14.7 19.6 %collective-permute-start.12 = (s32[1,256]{1,0:T(1,128)S(1)}, s32[1,256]{1,0:T(1,128)S(1)}, u32[]{:S(2)}, u32[]{:S(2)}) collective-permute-start(s32[1,256]{1,0:T(1,128)S(1)} %bitcast.16), channel_id=1, source_target_pairs={{20,0},{16,4},{28,8},{24,12},{4,16},{0,20},{12,24},{8,28},{21,1},{... | collective-permute-start | bytes 3080 | tf_op jit(solution)/shard_map/ppermute | solution.py:382
  15.1 19.3 %collective-permute-start.11 = (s32[1,256]{1,0:T(1,128)S(1)}, s32[1,256]{1,0:T(1,128)S(1)}, u32[]{:S(2)}, u32[]{:S(2)}) collective-permute-start(s32[1,256]{1,0:T(1,128)S(1)} %bitcast.17), channel_id=1, source_target_pairs={{16,0},{20,4},{24,8},{28,12},{0,16},{4,20},{8,24},{12,28},{17,1},{... | collective-permute-start | bytes 3080 | tf_op jit(solution)/shard_map/ppermute | solution.py:382
  17.4 16.9 %collective-permute-start.10 = (s32[1,256]{1,0:T(1,128)S(1)}, s32[1,256]{1,0:T(1,128)S(1)}, u32[]{:S(2)}, u32[]{:S(2)}) collective-permute-start(s32[1,256]{1,0:T(1,128)S(1)} %bitcast.18), channel_id=1, source_target_pairs={{12,0},{8,4},{4,8},{0,12},{28,16},{24,20},{20,24},{16,28},{13,1},{... | collective-permute-start | bytes 3080 | tf_op jit(solution)/shard_map/ppermute | solution.py:382
  33.7 3.6 %collective-permute-start.9 = (s32[1,256]{1,0:T(1,128)S(1)}, s32[1,256]{1,0:T(1,128)S(1)}, u32[]{:S(2)}, u32[]{:S(2)}) collective-permute-start(s32[1,256]{1,0:T(1,128)S(1)} %bitcast.19), channel_id=1, source_target_pairs={{8,0},{12,4},{0,8},{4,12},{24,16},{28,20},{16,24},{20,28},{9,1},{1... | collective-permute-start | bytes 3080 | tf_op jit(solution)/shard_map/ppermute | solution.py:382
  33.7 3.6 %collective-permute-start.8 = (s32[1,256]{1,0:T(1,128)S(1)}, s32[1,256]{1,0:T(1,128)S(1)}, u32[]{:S(2)}, u32[]{:S(2)}) collective-permute-start(s32[1,256]{1,0:T(1,128)S(1)} %bitcast.20), channel_id=1, source_target_pairs={{4,0},{0,4},{12,8},{8,12},{20,16},{16,20},{28,24},{24,28},{5,1},{1... | collective-permute-start | bytes 3080 | tf_op jit(solution)/shard_map/ppermute | solution.py:382

commit v2 on v1

--- a/solution.py
+++ b/solution.py
@@ -17,6 +17,7 @@
 EXP_SCALE = ATTN_SCALE * 1.4426950408889634
 HIDDEN = -1e30
 TOGETHER = 2
+SPLITS = 4
 TILE = 256
 F32 = jnp.float32
 BF16 = jnp.bfloat16
@@ -32,7 +33,7 @@
 def pack_kernel(groups, q_ref, g_ref, k_ref, v_ref, out_ref, q_sc, g_sc, k_sc, v_sc, hold, in_sem, out_sem):
     qw = PER_GROUP * HEAD_DIM
     kw = HEAD_DIM
-    half = groups // 2
+    half = groups // SPLITS
     pairs = ((q_ref, q_sc, qw, 0), (g_ref, g_sc, qw, qw), (k_ref, k_sc, kw, 2 * qw), (v_ref, v_sc, kw, 2 * qw + kw))
 
     def fetch(part):
@@ -48,10 +49,10 @@
     def emit(j):
         return pltpu.make_async_copy(hold.at[j], out_ref.at[j], out_sem.at[j])
 
-    for part in range(2):
+    for part in range(SPLITS):
         for copy in fetch(part):
             copy.start()
-    for part in range(2):
+    for part in range(SPLITS):
         for copy in fetch(part):
             copy.wait()
         for j in range(part * half, (part + 1) * half):
@@ -117,6 +118,19 @@
             dkt_sc[:, at] += dk
             dvt_sc[:, at] += dv
 
+    def own_scores(i, t, held):
+        at = slice(t * TILE, (t + 1) * TILE)
+        span = slice(i * TILE, (i + 1) * TILE)
+        q = jnp.concatenate([x_ref[span, n * d : (n + 1) * d] for n in range(PER_GROUP)], 0)
+        low = jnp.concatenate([low_all[i : i + 1]] * PER_GROUP, 1)
+        s = dot(x_ref[at, key_at : key_at + d], q, ((1,), (1,)))
+        s = jnp.where(key_rows >= low - t * TILE, s, HIDDEN)
+        if t == i:
+            s = jnp.where(key_rows <= lanes, s, HIDDEN)
+        s_sc[i % 2, at, :] = s
+        held[0] = jnp.maximum(held[0], jnp.max(s, axis=0, keepdims=True))
+
+    ahead = None
     for i in range(q_tiles):
         span = slice(i * TILE, (i + 1) * TILE)
         cols = slice(i * wide, (i + 1) * wide)
@@ -129,15 +143,11 @@
         low = jnp.concatenate([low_all[i : i + 1]] * PER_GROUP, 1)
         first = jnp.maximum(bounds_ref[i] + prev_tiles, 0)
 
-        top = jnp.full((1, wide), HIDDEN, F32)
-        for t in range(i + 1):
-            at = slice(t * TILE, (t + 1) * TILE)
-            s = dot(x_ref[at, key_at : key_at + d], q, ((1,), (1,)))
-            s = jnp.where(key_rows >= low - t * TILE, s, HIDDEN)
-            if t == i:
-                s = jnp.where(key_rows <= lanes, s, HIDDEN)
-            s_sc[at, :] = s
-            top = jnp.maximum(top, jnp.max(s, axis=0, keepdims=True))
+        if i == 0 or prev:
+            ahead = [jnp.full((1, wide), HIDDEN, F32)]
+            for t in range(i + 1):
+                own_scores(i, t, ahead)
+        top = ahead[0]
 
         def scores(t, top):
             s = dot(kp_sc[t], q, ((1,), (1,)))
@@ -151,7 +161,7 @@
 
         for t in range(i + 1):
             at = slice(t * TILE, (t + 1) * TILE)
-            e = jnp.exp2(s_sc[at, :] * EXP_SCALE - shift)
+            e = jnp.exp2(s_sc[i % 2, at, :] * EXP_SCALE - shift)
             e_sc[at, cols] = e.astype(BF16)
             if t < i:
                 collect(i - 1, t)
@@ -177,10 +187,16 @@
         gs_sc[:, cols] = (gt * inverse).astype(BF16)
         qs_sc[:, cols] = (q.T.astype(F32) * (inverse * ATTN_SCALE)).astype(BF16)
 
+        held = [jnp.full((1, wide), HIDDEN, F32)]
         for t in range(i + 1):
             at = slice(t * TILE, (t + 1) * TILE)
             dp = dot(x_ref[at, value_at : value_at + d], g, ((1,), (1,)))
             ds_sc[at, cols] = e_sc[at, cols] * (dp - delta).astype(BF16)
+            if not prev and i + 1 < q_tiles:
+                own_scores(i + 1, t, held)
+        if not prev and i + 1 < q_tiles:
+            own_scores(i + 1, i + 1, held)
+            ahead = held
         dq = dot(kt_sc[:, reach], ds_sc[reach, cols], ((1,), (0,)))
 
         def backward(t, carry):
@@ -294,7 +310,7 @@
     own_scratch = [
         pltpu.VMEM((d, rows), BF16),
         pltpu.VMEM((d + 16, rows), BF16),
-        pltpu.VMEM((rows, wide), F32),
+        pltpu.VMEM((2, rows, wide), F32),
         pltpu.VMEM((rows, span), BF16),
         pltpu.VMEM((rows, span), BF16),
         pltpu.VMEM((d, span), BF16),
@@ -360,7 +376,7 @@
             pltpu.VMEM(keys.shape, BF16),
             pltpu.VMEM(keys.shape, BF16),
             pltpu.VMEM((groups, local, 2 * qw + 2 * d), BF16),
-            pltpu.SemaphoreType.DMA((2, 4)),
+            pltpu.SemaphoreType.DMA((SPLITS, 4)),
             pltpu.SemaphoreType.DMA((groups,)),
         ],
     )(queries, grad_out, keys, values)
@@ -378,6 +394,7 @@
                 (((b - back) % blocks) * subs + (s ^ turn), b * subs + s)
                 for b in range(blocks)
                 for s in range(subs)
+                if b or not back or s == turn
             ]
             parts.append(lax.ppermute(line, both, route) if back or turn else line)
         return parts

time: 73.4 us -> 69.7 us (0.950)
  the two profiles are of different devices: /device:TPU:0 before, /device:TPU:16 now
where the time goes in v2:
time: 69.7 us; the launch traced here: 69.3 us
  starting transfers between devices  27.2 us (39%)
  blocking collectives  26.1 us (37%)
  Pallas kernels  11.3 us (16%)
  waiting for transfers between devices  3.15 us (5%)
  between operations  1.35 us (2%)
    all_to_all x1, blocking collectives, swap(): return lax.all_to_all(value, ('sub', 'head'), 0, 0, tiled=True)  26.1 us
    ppermute x7, starting transfers between devices, turned_ids(): parts.append(lax.ppermute(line, both, route) if back or turn else line)  22.3 us
    pallas_call x1, Pallas kernels, attend(): pl.pallas_call(kernel, out_shape=out_shape, in_specs=[SCALARS] + [WHOLE]...  6.08 us
    all_to_all x1, starting transfers between devices, body(): lax.all_to_all(packed, ('sub', 'head'), 0, 0, tiled=True)  4.85 us
    ppermute x7, waiting for transfers between devices, turned_ids(): parts.append(lax.ppermute(line, both, route) if back or turn else line)  3.15 us
    pallas_call x1, Pallas kernels, body(): pl.pallas_call(lambda *refs: pack_kernel(groups, *refs), name='pack', out...  2.52 us
  transfers between devices with their start and end apart: 8, of which 2 were waited for; matrix products, arithmetic and copies ran while one was open for 0% of the time, Pallas kernels for 2%

profile of v2, /device:TPU:16, one launch (start us, length us, event | category | flops | bytes accessed | tf_op | source)
XLA Modules:
  0.0 69.3 jit_solution(3071608650132828397)
XLA Ops:
  0.6 2.5 %pack.1 = bf16[16,64,768]{2,1,0:T(8,128)(2,1)} custom-call(bf16[64,4096]{1,0:T(8,128)(2,1)} %refs_0_.1, bf16[64,4096]{1,0:T(8,128)(2,1)} %refs_1_.1, bf16[64,2048]{1,0:T(8,128)(2,1)} %refs_2_.1, bf16[64,2048]{1,0:T(8,128)(2,1)} %refs_3_.1), custom_call_target="tpu_custom_call" | custom-call | tf_op jit(solution)/shard_map/pack/pallas_call | solution.py:367
  3.2 0.0 copy-start
  3.2 4.9 %all-to-all-start.8 = ((bf16[16,64,768]{2,1,0:T(8,128)(2,1)}), bf16[16,64,768]{2,1,0:T(8,128)(2,1)S(1)}, u32[]{:S(2)}, u32[]{:S(2)}) async-start(bf16[16,64,768]{2,1,0:T(8,128)(2,1)} %pack.1), calls=%async_computation.8 | async-start | bytes 3145728 | tf_op jit(solution)/shard_map/all_to_all | solution.py:383
  8.0 0.0 copy-done
  8.0 3.6 %collective-permute-start.14 = (s32[1,256]{1,0:T(1,128)S(1)}, s32[1,256]{1,0:T(1,128)S(1)}, u32[]{:S(2)}, u32[]{:S(2)}) collective-permute-start(s32[1,256]{1,0:T(1,128)S(1)} %bitcast.14), channel_id=1, source_target_pairs={{16,12},{12,16},{8,20},{4,24},{0,28},{17,13},{13,17},{9,21},{5,25}... | collective-permute-start | bytes 3080 | tf_op jit(solution)/shard_map/ppermute | solution.py:399
  11.7 3.6 %collective-permute-start.13 = (s32[1,256]{1,0:T(1,128)S(1)}, s32[1,256]{1,0:T(1,128)S(1)}, u32[]{:S(2)}, u32[]{:S(2)}) collective-permute-start(s32[1,256]{1,0:T(1,128)S(1)} %bitcast.15), channel_id=1, source_target_pairs={{16,8},{8,16},{12,20},{0,24},{4,28},{17,9},{9,17},{13,21},{1,25},{... | collective-permute-start | bytes 3080 | tf_op jit(solution)/shard_map/ppermute | solution.py:399
  15.3 3.1 %collective-permute-start.12 = (s32[1,256]{1,0:T(1,128)S(1)}, s32[1,256]{1,0:T(1,128)S(1)}, u32[]{:S(2)}, u32[]{:S(2)}) collective-permute-start(s32[1,256]{1,0:T(1,128)S(1)} %bitcast.16), channel_id=1, source_target_pairs={{16,4},{4,16},{0,20},{12,24},{8,28},{17,5},{5,17},{1,21},{13,25},{... | collective-permute-start | bytes 3080 | tf_op jit(solution)/shard_map/ppermute | solution.py:399
  18.4 1.9 %collective-permute-start.11 = (s32[1,256]{1,0:T(1,128)S(1)}, s32[1,256]{1,0:T(1,128)S(1)}, u32[]{:S(2)}, u32[]{:S(2)}) collective-permute-start(s32[1,256]{1,0:T(1,128)S(1)} %bitcast.17), channel_id=1, source_target_pairs={{16,0},{0,16},{4,20},{8,24},{12,28},{17,1},{1,17},{5,21},{9,25},{1... | collective-permute-start | bytes 3080 | tf_op jit(solution)/shard_map/ppermute | solution.py:399
  20.3 0.1 collective-permute-start.10
  20.4 0.0 collective-permute-done.14.refs_8_
  20.4 9.7 %collective-permute-start.9 = (s32[1,256]{1,0:T(1,128)S(1)}, s32[1,256]{1,0:T(1,128)S(1)}, u32[]{:S(2)}, u32[]{:S(2)}) collective-permute-start(s32[1,256]{1,0:T(1,128)S(1)} %bitcast.19), channel_id=1, source_target_pairs={{8,0},{12,4},{0,8},{4,12},{24,16},{28,20},{16,24},{20,28},{9,1},{1... | collective-permute-start | bytes 3080 | tf_op jit(solution)/shard_map/ppermute | solution.py:399
  30.0 0.0 collective-permute-done.13.refs_7_
  30.0 0.4 collective-permute-start.8
  30.4 0.1 pad_add_fusion.refs_0_
  30.5 0.0 collective-permute-done.12.refs_6_
  30.5 0.0 collective-permute-done.11.refs_5_
  30.5 0.0 collective-permute-done.10.refs_4_
  30.5 1.1 %collective-permute-done.9.refs_3_ = s32[1,256]{1,0:T(1,128)S(1)} collective-permute-done((s32[1,256]{1,0:T(1,128)S(1)}, s32[1,256]{1,0:T(1,128)S(1)}, u32[]{:S(2)}, u32[]{:S(2)}) %collective-permute-start.9) | collective-permute-done | bytes 1056 | tf_op jit(solution)/shard_map/ppermute | solution.py:399
  31.6 2.0 %collective-permute-done.8.refs_2_ = s32[1,256]{1,0:T(1,128)S(1)} collective-permute-done((s32[1,256]{1,0:T(1,128)S(1)}, s32[1,256]{1,0:T(1,128)S(1)}, u32[]{:S(2)}, u32[]{:S(2)}) %collective-permute-start.8) | collective-permute-done | bytes 1056 | tf_op jit(solution)/shard_map/ppermute | solution.py:399
  33.6 1.4 %decide.1 = (f32[8,256]{1,0:T(8,128)S(1)}, s32[9]{0:T(128)S(1)}, s32[1]{0:T(128)}) custom-call(s32[2]{0:T(128)S(1)} %pad_add_fusion.refs_0_, s32[1,256]{1,0:T(1,128)S(1)} %bitcast.21, s32[1,256]{1,0:T(1,128)S(1)} %collective-permute-done.8.refs_2_, s32[1,256]{1,0:T(1,128)S(1)} %collective-permute-done.9.refs_3_, ...), custom_call_target="tpu_custom_call" | custom-call | tf_op jit(solution)/shard_map/decide/pallas_call | solution.py:403
  35.6 0.0 all-to-all-done.8
  35.6 33.7 %conditional.3 = ((bf16[64,4096]{1,0:T(8,128)(2,1)}, bf16[64,4096]{1,0:T(8,128)(2,1)}, bf16[64,2048]{1,0:T(8,128)(2,1)}, bf16[64,2048]{1,0:T(8,128)(2,1)})) conditional(s32[]{:T(128)} %convert_element_type.33, (s32[]{:T(128)}, bf16[1024,768]{1,0:T(8,128)(2,1)S(1)}, s32[9]{0:T(128)S(1)}, f32[8,256]{1,0:T(8,128)S(1)}) %tuple.63, (s32[9]{0:T(128)S(1)}, ...), branch_computations={%region_0.9_spmd, %region_9.10_spmd} | conditional | flops 3932164 | bytes 12058822 | solution.py:478
  35.8 6.1 %branch_1_fun.1 = bf16[1024,768]{1,0:T(8,128)(2,1)S(1)} custom-call(s32[9]{0:T(128)S(1)} %get-tuple-element.66.refs_0_, f32[8,256]{1,0:T(8,128)S(1)} %get-tuple-element.67.refs_1_, bf16[1024,768]{1,0:T(8,128)(2,1)S(1)} %get-tuple-element.68.refs_2_), custom_call_target="tpu_custom_call" | custom-call | tf_op jit(solution)/shard_map/cond/branch_1_fun/pallas_call | solution.py:347
  41.9 26.1 %all_to_all.44.refs_0_ = bf16[16,64,768]{2,1,0:T(8,128)(2,1)S(1)} all-to-all(bf16[16,64,768]{2,1,0:T(8,128)(2,1)S(1)} %bitcast.13), channel_id=1, replica_groups=mesh['block'=2,'sub'=4,'head'=4] {'sub','head'}, dimensions={0} | all-to-all | bytes 3145728 | tf_op jit(solution)/shard_map/cond/branch_1_fun/all_to_all | solution.py:424
  68.0 1.4 %unpack.9 = (bf16[64,4096]{1,0:T(8,128)(2,1)}, bf16[64,4096]{1,0:T(8,128)(2,1)}, bf16[64,2048]{1,0:T(8,128)(2,1)}, bf16[64,2048]{1,0:T(8,128)(2,1)}) custom-call(bf16[16,64,768]{2,1,0:T(8,128)(2,1)S(1)} %all_to_all.44.refs_0_), custom_call_target="tpu_custom_call" | custom-call | tf_op jit(solution)/shard_map/cond/branch_1_fun/unpack/pallas_call | solution.py:427
Async XLA Ops:
  3.2 4.9 %copy-start = (s32[256]{0:T(256)S(1)}, s32[256]{0:T(256)}, u32[]{:S(2)}) copy-start(s32[256]{0:T(256)} %param.19) | copy-start | bytes 3076
  3.2 32.5 %all-to-all-start.8 = ((bf16[16,64,768]{2,1,0:T(8,128)(2,1)}), bf16[16,64,768]{2,1,0:T(8,128)(2,1)S(1)}, u32[]{:S(2)}, u32[]{:S(2)}) async-start(bf16[16,64,768]{2,1,0:T(8,128)(2,1)} %pack.1), calls=%async_computation.8 | async-start | bytes 3145728 | tf_op jit(solution)/shard_map/all_to_all | solution.py:383
  8.0 12.3 %collective-permute-start.14 = (s32[1,256]{1,0:T(1,128)S(1)}, s32[1,256]{1,0:T(1,128)S(1)}, u32[]{:S(2)}, u32[]{:S(2)}) collective-permute-start(s32[1,256]{1,0:T(1,128)S(1)} %bitcast.14), channel_id=1, source_target_pairs={{16,12},{12,16},{8,20},{4,24},{0,28},{17,13},{13,17},{9,21},{5,25}... | collective-permute-start | bytes 3080 | tf_op jit(solution)/shard_map/ppermute | solution.py:399
  11.7 18.4 %collective-permute-start.13 = (s32[1,256]{1,0:T(1,128)S(1)}, s32[1,256]{1,0:T(1,128)S(1)}, u32[]{:S(2)}, u32[]{:S(2)}) collective-permute-start(s32[1,256]{1,0:T(1,128)S(1)} %bitcast.15), channel_id=1, source_target_pairs={{16,8},{8,16},{12,20},{0,24},{4,28},{17,9},{9,17},{13,21},{1,25},{... | collective-permute-start | bytes 3080 | tf_op jit(solution)/shard_map/ppermute | solution.py:399
  15.3 15.2 %collective-permute-start.12 = (s32[1,256]{1,0:T(1,128)S(1)}, s32[1,256]{1,0:T(1,128)S(1)}, u32[]{:S(2)}, u32[]{:S(2)}) collective-permute-start(s32[1,256]{1,0:T(1,128)S(1)} %bitcast.16), channel_id=1, source_target_pairs={{16,4},{4,16},{0,20},{12,24},{8,28},{17,5},{5,17},{1,21},{13,25},{... | collective-permute-start | bytes 3080 | tf_op jit(solution)/shard_map/ppermute | solution.py:399
  18.4 12.1 %collective-permute-start.11 = (s32[1,256]{1,0:T(1,128)S(1)}, s32[1,256]{1,0:T(1,128)S(1)}, u32[]{:S(2)}, u32[]{:S(2)}) collective-permute-start(s32[1,256]{1,0:T(1,128)S(1)} %bitcast.17), channel_id=1, source_target_pairs={{16,0},{0,16},{4,20},{8,24},{12,28},{17,1},{1,17},{5,21},{9,25},{1... | collective-permute-start | bytes 3080 | tf_op jit(solution)/shard_map/ppermute | solution.py:399
  20.3 10.2 %collective-permute-start.10 = (s32[1,256]{1,0:T(1,128)S(1)}, s32[1,256]{1,0:T(1,128)S(1)}, u32[]{:S(2)}, u32[]{:S(2)}) collective-permute-start(s32[1,256]{1,0:T(1,128)S(1)} %bitcast.18), channel_id=1, source_target_pairs={{12,0},{8,4},{4,8},{0,12},{28,16},{24,20},{20,24},{16,28},{13,1},{... | collective-permute-start | bytes 3080 | tf_op jit(solution)/shard_map/ppermute | solution.py:399
  20.4 11.2 %collective-permute-start.9 = (s32[1,256]{1,0:T(1,128)S(1)}, s32[1,256]{1,0:T(1,128)S(1)}, u32[]{:S(2)}, u32[]{:S(2)}) collective-permute-start(s32[1,256]{1,0:T(1,128)S(1)} %bitcast.19), channel_id=1, source_target_pairs={{8,0},{12,4},{0,8},{4,12},{24,16},{28,20},{16,24},{20,28},{9,1},{1... | collective-permute-start | bytes 3080 | tf_op jit(solution)/shard_map/ppermute | solution.py:399
  30.0 3.6 %collective-permute-start.8 = (s32[1,256]{1,0:T(1,128)S(1)}, s32[1,256]{1,0:T(1,128)S(1)}, u32[]{:S(2)}, u32[]{:S(2)}) collective-permute-start(s32[1,256]{1,0:T(1,128)S(1)} %bitcast.20), channel_id=1, source_target_pairs={{4,0},{0,4},{12,8},{8,12},{20,16},{16,20},{28,24},{24,28},{5,1},{1... | collective-permute-start | bytes 3080 | tf_op jit(solution)/shard_map/ppermute | solution.py:399
